TPU v7x, 512 devices: a whole 4x8x8 slice. The times are simulated.
512 devices in a mesh: dom: 128 (over y, z, core), rep: 4 (over x).
Axes of the slice: x: 4, y: 8, z: 8, core: 2. Of those that a mesh axis runs over, the one named last changes fastest.
Arguments:
- feats: bfloat16 [131072, 256], P('dom'), may hold values from -6 to 6
- history: bfloat16 [131072, 256], P('dom'), may hold values from -6 to 6
- adj_inner: bfloat16 [131072, 1024], P('dom'), may hold values from -0.15625 to 0.15625
- adj_halo: bfloat16 [131072, 256], P('dom'), may hold values from -0.15625 to 0.15625
- halo_rows: int32 [16384, 2], P('dom'), may hold values from 0 to 1023
- w_self: bfloat16 [256, 256], replicated, may hold values from -0.375 to 0.375
- w_nbr: bfloat16 [256, 256], replicated, may hold values from -0.375 to 0.375
- b_enc: float32 [256], replicated, may hold values from -3 to 3
- edge_owner: int32 [131072, 2], P(('dom', 'rep')), may hold values from 0 to 127, all different within a row; in each aligned block of 256 rows (0 to 255, 256 to 511, ...) at most 8 rows name the same one
- edge_rows: int32 [131072, 2], P(('dom', 'rep')), may hold values from 0 to 1023
- labels: int32 [131072], P(('dom', 'rep')), may hold values 0 or 1
- w_dec1: bfloat16 [256, 256], replicated, may hold values from -0.375 to 0.375
- b_dec1: float32 [256], replicated, may hold values from -3 to 3
- w_dec2: bfloat16 [256], replicated, may hold values from -0.375 to 0.375
Outputs:
- embed: bfloat16 [131072, 256], P('dom')
- grad_embed: float32 [131072, 256], P(('dom', 'rep'))
- grad_dec1: float32 [256, 256], replicated
- grad_bias1: float32 [256], replicated
- grad_dec2: float32 [256], replicated
Inputs may be any that keep to these rules, and one draw needn't show every extreme that they name: `edge_owner`: among the rows of one device, no owner is named by more than 8 endpoints, a bound that some block reaches; the two endpoints of an edge have different owners.
All inputs are finite; a program needn't handle non-finite values. No bound on the sum of `labels` on one device may be relied on, other than what follows from the above.
Results may differ from a plain program's by a relative error of at most 0.0069.
Values may be sent and summed in bfloat16 or wider, within the bound.
A program may use at most 64 MiB of HBM per device.

v0:
```python
import jax
import jax.numpy as jnp
from jax import lax
from jax.sharding import PartitionSpec as P


def encode_block(rows_x, a_inner, a_halo, all_x, halo, w_self, w_nbr, b_enc):
    agg = (
        jnp.dot(a_inner, all_x, preferred_element_type=jnp.float32)
        + jnp.dot(a_halo, halo, preferred_element_type=jnp.float32)
    ).astype(jnp.bfloat16)
    pre = (
        jnp.dot(rows_x, w_self, preferred_element_type=jnp.float32)
        + jnp.dot(agg, w_nbr, preferred_element_type=jnp.float32)
        + b_enc
    )
    return jnp.maximum(pre, 0.0).astype(jnp.bfloat16)


def decode(head, tail, target, w_dec1, b_dec1, w_dec2):
    zprod = (head.astype(jnp.float32) * tail.astype(jnp.float32)).astype(jnp.bfloat16)
    pre = jnp.dot(zprod, w_dec1, preferred_element_type=jnp.float32) + b_dec1
    sig = jax.nn.sigmoid(pre)
    hidden = (pre * sig).astype(jnp.bfloat16)
    logit = jnp.dot(hidden, w_dec2, preferred_element_type=jnp.float32)
    dlogit = jax.nn.sigmoid(logit) - target
    d_pre = (
        dlogit[:, None] * w_dec2.astype(jnp.float32) * (sig * (1.0 + pre * (1.0 - sig)))
    ).astype(jnp.bfloat16)
    grad_w1 = jnp.dot(zprod.T, d_pre, preferred_element_type=jnp.float32)
    grad_b1 = jnp.sum(d_pre.astype(jnp.float32), axis=0)
    grad_w2 = jnp.sum(hidden.astype(jnp.float32) * dlogit[:, None], axis=0)
    dzval = jnp.dot(d_pre, w_dec1.T, preferred_element_type=jnp.float32)
    return (
        dzval * tail.astype(jnp.float32),
        dzval * head.astype(jnp.float32),
        grad_w1,
        grad_b1,
        grad_w2,
    )


def per_device(
    feats,
    history,
    adj_inner,
    adj_halo,
    halo_rows,
    w_self,
    w_nbr,
    b_enc,
    edge_owner,
    edge_rows,
    labels,
    w_dec1,
    b_dec1,
    w_dec2,
):
    n_dom = lax.axis_size("dom")
    nodes = feats.shape[0]
    width = feats.shape[1]
    halo = lax.all_to_all(
        history[lax.all_to_all(halo_rows, "dom", split_axis=0, concat_axis=0, tiled=True)],
        "dom",
        split_axis=0,
        concat_axis=0,
        tiled=True,
    ).reshape(-1, width)
    embed = encode_block(feats, adj_inner, adj_halo, feats, halo, w_self, w_nbr, b_enc)
    queries = edge_owner.shape[0]
    cap_edge = max(2, 4 * queries // n_dom)
    owners = edge_owner.reshape(-1)
    local = edge_rows.reshape(-1)
    match = (owners[:, None] == jnp.arange(n_dom, dtype=jnp.int32)[None, :]).astype(jnp.int32)
    slots = jnp.sum(jnp.cumsum(match, axis=0) * match, axis=1) - 1
    place = owners * cap_edge + slots
    send_ids = (
        jnp.zeros((n_dom * cap_edge,), jnp.int32).at[place].set(local).reshape(n_dom, cap_edge)
    )
    wanted = lax.all_to_all(send_ids, "dom", split_axis=0, concat_axis=0, tiled=True)
    fetched = lax.all_to_all(embed[wanted], "dom", split_axis=0, concat_axis=0, tiled=True)
    ends = fetched.reshape(-1, width)[place].reshape(queries, 2, width)
    target = labels.astype(jnp.float32)
    g_head, g_tail, gw1, gb1, gw2 = decode(ends[:, 0], ends[:, 1], target, w_dec1, b_dec1, w_dec2)
    grads = jnp.stack([g_head, g_tail], axis=1).reshape(-1, width)
    send_grads = jnp.zeros((n_dom * cap_edge, width), jnp.float32).at[place].set(grads)
    back = lax.all_to_all(
        send_grads.reshape(n_dom, cap_edge, width), "dom", split_axis=0, concat_axis=0, tiled=True
    )
    local_grad = (
        jnp.zeros((nodes, width), jnp.float32).at[wanted.reshape(-1)].add(back.reshape(-1, width))
    )
    grad_embed = lax.psum_scatter(local_grad, "rep", scatter_dimension=0, tiled=True)
    grad_dec1, grad_bias1, grad_dec2 = lax.psum((gw1, gb1, gw2), ("dom", "rep"))
    return (embed, grad_embed, grad_dec1, grad_bias1, grad_dec2)


def solution(mesh):
    placed = (
        P("dom", None),
        P("dom", None),
        P("dom", None),
        P("dom", None),
        P("dom", None),
        P(),
        P(),
        P(),
        P(("dom", "rep"), None),
        P(("dom", "rep"), None),
        P(("dom", "rep")),
        P(),
        P(),
        P(),
    )
    return jax.shard_map(
        per_device,
        mesh=mesh,
        in_specs=placed,
        out_specs=(P("dom", None), P(("dom", "rep"), None), P(), P(), P()),
        check_vma=False,
    )
```

profile of v0, /device:TPU:23, one launch (start us, length us, event | category | flops | bytes accessed | tf_op | source)
XLA Modules:
  0.0 414.1 jit_solution(18180660561444571792)
XLA Ops:
  8.0 1.6 copy.30
  9.6 17.7 %all-to-all-start = ((s32[128,1,2]{2,1,0:T(1,128)}), s32[128,1,2]{2,1,0:T(1,128)S(1)}, u32[]{:S(2)}, u32[]{:S(2)}) async-start(s32[128,1,2]{2,1,0:T(1,128)} %bitcast), calls=%async_computation | async-start | bytes 131072 | tf_op jit(solution)/shard_map/all_to_all | solution.py:63
  27.9 0.8 copy.33
  30.1 1.7 fusion.21
  31.8 1.3 fusion.20
  33.4 2.4 scatter_custom_fusion
  37.0 13.3 %all-to-all-start.2 = ((s32[128,1,8]{2,1,0:T(1,128)}), s32[128,1,8]{2,1,0:T(1,128)S(1)}, u32[]{:S(2)}, u32[]{:S(2)}) async-start(s32[128,1,8]{2,1,0:T(1,128)} %bitcast.8), calls=%async_computation.2 | async-start | bytes 131072 | tf_op jit(solution)/shard_map/all_to_all | solution.py:80
  50.5 1.2 gather_fusion
  52.4 7.7 %all-to-all-done.2 = s32[128,1,8]{2,1,0:T(1,128)S(1)} async-done(((s32[128,1,8]{2,1,0:T(1,128)}), s32[128,1,8]{2,1,0:T(1,128)S(1)}, u32[]{:S(2)}, u32[]{:S(2)}) %all-to-all-start.2) | async-done | bytes 4128 | tf_op jit(solution)/shard_map/all_to_all | solution.py:80
  60.1 7.5 %all-to-all-start.1 = ((bf16[128,2,256]{2,1,0:T(2,128)(2,1)}), bf16[128,2,256]{2,1,0:T(2,128)(2,1)S(1)}, u32[]{:S(2)}, u32[]{:S(2)}) async-start(bf16[128,2,256]{2,1,0:T(2,128)(2,1)} %reshape.196), calls=%async_computation.1 | async-start | bytes 262144 | tf_op jit(solution)/shard_map/all_to_all | solution.py:62
  67.8 11.0 %all-to-all-done.1 = bf16[128,2,256]{2,1,0:T(2,128)(2,1)S(1)} async-done(((bf16[128,2,256]{2,1,0:T(2,128)(2,1)}), bf16[128,2,256]{2,1,0:T(2,128)(2,1)S(1)}, u32[]{:S(2)}, u32[]{:S(2)}) %all-to-all-start.1) | async-done | bytes 131104 | tf_op jit(solution)/shard_map/all_to_all | solution.py:62
  78.8 2.2 fusion.3
  81.0 5.0 %gather_fusion.1 = bf16[1024,256]{1,0:T(8,128)(2,1)} fusion(bf16[1024,256]{1,0:T(8,128)(2,1)S(1)} %fusion.3, s32[1024]{0:T(1024)S(1)} %broadcast_clamp_fusion), kind=kCustom, calls=%fused_computation.1 | custom fusion | bytes 1052672 | tf_op jit(solution)/shard_map/gather | solution.py:81
  86.0 7.5 %all-to-all-start.3 = ((bf16[128,8,256]{2,1,0:T(8,128)(2,1)}), bf16[128,8,256]{2,1,0:T(8,128)(2,1)S(1)}, u32[]{:S(2)}, u32[]{:S(2)}) async-start(bf16[128,8,256]{2,1,0:T(8,128)(2,1)} %bitcast.11), calls=%async_computation.3 | async-start | bytes 1048576 | tf_op jit(solution)/shard_map/all_to_all | solution.py:81
  93.6 17.8 %all-to-all-done.3 = bf16[128,8,256]{2,1,0:T(8,128)(2,1)S(1)} async-done(((bf16[128,8,256]{2,1,0:T(8,128)(2,1)}), bf16[128,8,256]{2,1,0:T(8,128)(2,1)S(1)}, u32[]{:S(2)}, u32[]{:S(2)}) %all-to-all-start.3) | async-done | bytes 524320 | tf_op jit(solution)/shard_map/all_to_all | solution.py:81
  111.4 1.9 gather_fusion.2
  115.6 3.2 scatter_custom_fusion.1
  118.9 8.8 %all-to-all-start.4 = ((f32[128,8,256]{2,1,0:T(8,128)}), f32[128,8,256]{2,1,0:T(8,128)S(1)}, u32[]{:S(2)}, u32[]{:S(2)}) async-start(f32[128,8,256]{2,1,0:T(8,128)} %bitcast.73), calls=%async_computation.4 | async-start | bytes 2097152 | tf_op jit(solution)/shard_map/all_to_all | solution.py:87
  129.2 0.9 fusion.23
  130.2 26.3 %all-to-all-done.4 = f32[128,8,256]{2,1,0:T(8,128)S(1)} async-done(((f32[128,8,256]{2,1,0:T(8,128)}), f32[128,8,256]{2,1,0:T(8,128)S(1)}, u32[]{:S(2)}, u32[]{:S(2)}) %all-to-all-start.4) | async-done | bytes 1048608 | tf_op jit(solution)/shard_map/all_to_all | solution.py:87
  156.5 7.1 %scatter_custom_fusion.2 = f32[1024,256]{1,0:T(8,128)} fusion(s32[1024]{0:T(1024)S(1)} %bitcast.84, f32[128,8,256]{2,1,0:T(8,128)S(1)} %all-to-all-done.4, f32[]{:T(128)} %constant.8.clone.1), kind=kCustom, calls=%fused_computation.14 | custom fusion | flops 262144 | bytes 2097156 | tf_op jit(solution)/shard_map/scatter-add | solution.py:91
  163.6 95.2 %all-reduce = (f32[256]{0:T(256)}, f32[256]{0:T(256)}) all-reduce(f32[256]{0:T(256)S(1)} %get-tuple-element.7, f32[256]{0:T(256)S(1)} %get-tuple-element.13), channel_id=1, replica_groups=mesh['dom'=128,'rep'=4] {'dom','rep'}, use_global_device_ids=true, to_apply=%region_9.10 | all-reduce | flops 512 | bytes 4096 | tf_op jit(solution)/shard_map/psum | solution.py:94
  258.9 146.1 %all-reduce.3.cloned.1.call-done = f32[256,256]{1,0:T(8,128)} async-done(((f32[256,256]{1,0:T(8,128)}), f32[256,256]{1,0:T(8,128)}) %all-reduce.3.cloned.1.call-update) | async-done | bytes 262160 | tf_op jit(solution)/shard_map/psum | solution.py:94
  404.9 1.7 copy.56
  (77 shorter events, 8.1 us)
Async XLA Ops:
  8.0 22.0 %copy-start = (bf16[1024,1024]{1,0:T(8,128)(2,1)S(1)}, bf16[1024,1024]{1,0:T(8,128)(2,1)}, u32[]{:S(2)}) copy-start(bf16[1024,1024]{1,0:T(8,128)(2,1)} %param.16) | copy-start | bytes 6291460
  8.0 22.0 %copy-start.4 = (bf16[1024,256]{1,0:T(8,128)(2,1)S(1)}, bf16[1024,256]{1,0:T(8,128)(2,1)}, u32[]{:S(2)}) copy-start(bf16[1024,256]{1,0:T(8,128)(2,1)} %param.14) | copy-start | bytes 1572868
  9.6 27.4 %all-to-all-start = ((s32[128,1,2]{2,1,0:T(1,128)}), s32[128,1,2]{2,1,0:T(1,128)S(1)}, u32[]{:S(2)}, u32[]{:S(2)}) async-start(s32[128,1,2]{2,1,0:T(1,128)} %bitcast), calls=%async_computation | async-start | bytes 131072 | tf_op jit(solution)/shard_map/all_to_all | solution.py:63
  30.0 1.8 copy-start.5
  30.1 1.8 copy-start.6
  30.1 3.1 copy-start.8
  31.8 18.7 %copy-start.2 = (bf16[1024,256]{1,0:T(8,128)(2,1)S(1)}, bf16[1024,256]{1,0:T(8,128)(2,1)}, u32[]{:S(2)}) copy-start(bf16[1024,256]{1,0:T(8,128)(2,1)} %param.15) | copy-start | bytes 1572868
  31.8 47.0 %copy-start.3 = (bf16[1024,256]{1,0:T(8,128)(2,1)S(1)}, bf16[1024,256]{1,0:T(8,128)(2,1)}, u32[]{:S(2)}) copy-start(bf16[1024,256]{1,0:T(8,128)(2,1)} %param.17) | copy-start | bytes 1572868
  31.8 47.0 %copy-start.9 = (f32[256]{0:T(256)S(1)}, f32[256]{0:T(256)}, u32[]{:S(2)}) copy-start(f32[256]{0:T(256)} %param.21) | copy-start | bytes 3076
  37.0 23.1 %all-to-all-start.2 = ((s32[128,1,8]{2,1,0:T(1,128)}), s32[128,1,8]{2,1,0:T(1,128)S(1)}, u32[]{:S(2)}, u32[]{:S(2)}) async-start(s32[128,1,8]{2,1,0:T(1,128)} %bitcast.8), calls=%async_computation.2 | async-start | bytes 131072 | tf_op jit(solution)/shard_map/all_to_all | solution.py:80
  60.1 18.7 %all-to-all-start.1 = ((bf16[128,2,256]{2,1,0:T(2,128)(2,1)}), bf16[128,2,256]{2,1,0:T(2,128)(2,1)S(1)}, u32[]{:S(2)}, u32[]{:S(2)}) async-start(bf16[128,2,256]{2,1,0:T(2,128)(2,1)} %reshape.196), calls=%async_computation.1 | async-start | bytes 262144 | tf_op jit(solution)/shard_map/all_to_all | solution.py:62
  81.0 5.0 %copy-start.1 = (bf16[1024,256]{1,0:T(8,128)(2,1)}, bf16[1024,256]{1,0:T(8,128)(2,1)S(1)}, u32[]{:S(2)}) copy-start(bf16[1024,256]{1,0:T(8,128)(2,1)S(1)} %fusion.3) | copy-start | bytes 1572868
  81.0 12.5 %copy-start.12 = (bf16[256]{0:T(256)(128)(2,1)S(1)}, bf16[256]{0:T(256)(128)(2,1)}, u32[]{:S(2)}) copy-start(bf16[256]{0:T(256)(128)(2,1)} %param.27) | copy-start | bytes 1540
  86.0 25.4 %all-to-all-start.3 = ((bf16[128,8,256]{2,1,0:T(8,128)(2,1)}), bf16[128,8,256]{2,1,0:T(8,128)(2,1)S(1)}, u32[]{:S(2)}, u32[]{:S(2)}) async-start(bf16[128,8,256]{2,1,0:T(8,128)(2,1)} %bitcast.11), calls=%async_computation.3 | async-start | bytes 1048576 | tf_op jit(solution)/shard_map/all_to_all | solution.py:81
  111.4 2.5 copy-start.7
  111.4 2.5 copy-start.11
  113.4 1.0 copy-start.10
  118.9 37.6 %all-to-all-start.4 = ((f32[128,8,256]{2,1,0:T(8,128)}), f32[128,8,256]{2,1,0:T(8,128)S(1)}, u32[]{:S(2)}, u32[]{:S(2)}) async-start(f32[128,8,256]{2,1,0:T(8,128)} %bitcast.73), calls=%async_computation.4 | async-start | bytes 2097152 | tf_op jit(solution)/shard_map/all_to_all | solution.py:87
  127.7 277.2 %all-reduce.3.cloned.1.call-start = ((), (), s32[]{:S(2)}) async-start(), calls=%async_computation.7 | async-start | bytes 524288 | tf_op jit(solution)/shard_map/psum | solution.py:94
  130.2 274.8 %reduce-scatter.2.cloned.1.call-start = ((), (), s32[]{:S(2)}) async-start(), calls=%async_computation.6 | async-start | bytes 1310720 | tf_op jit(solution)/shard_map/reduce_scatter | solution.py:93
Sparse Core Ops, SparseCore 0:
  134.9 269.9 all-reduce.2
Sparse Core Ops, SparseCore 1:
  163.7 20.9 reduce-scatter.1
where the time goes:
time: 415 us; the launch traced here: 414 us
  waiting for transfers between devices  209 us (50%)
  blocking collectives  95.2 us (23%)
  starting transfers between devices  55 us (13%)
  local copies, waits for them, and re-layouts  22.4 us (5%)
  between operations  15.9 us (4%)
  other arithmetic  9.45 us (2%)
  matrix products  6.74 us (2%)
    psum x1, waiting for transfers between devices, per_device(): grad_dec1, grad_bias1, grad_dec2 = lax.psum((gw1, gb1, gw2), ('dom', 'rep'))  146 us
    psum x1, blocking collectives, per_device(): grad_dec1, grad_bias1, grad_dec2 = lax.psum((gw1, gb1, gw2), ('dom', 'rep'))  95.2 us
    all_to_all x1, waiting for transfers between devices, per_device(): lax.all_to_all(send_grads.reshape(n_dom, cap_edge, width), 'dom', split_a...  26.3 us
    all_to_all x1, waiting for transfers between devices, per_device(): lax.all_to_all(embed[wanted], 'dom', split_axis=0, concat_axis=0, tiled=T...  17.8 us
    all_to_all x1, starting transfers between devices, per_device(): lax.all_to_all(halo_rows, 'dom', split_axis=0, concat_axis=0, tiled=True)  17.7 us
    all_to_all x1, starting transfers between devices, per_device(): lax.all_to_all(send_ids, 'dom', split_axis=0, concat_axis=0, tiled=True)  13.3 us
    all_to_all x1, waiting for transfers between devices, per_device(): lax.all_to_all(history[lax.all_to_all(halo_rows, 'dom', split_axis=0, con...  11 us
    all_to_all x1, starting transfers between devices, per_device(): lax.all_to_all(send_grads.reshape(n_dom, cap_edge, width), 'dom', split_a...  8.84 us
  transfers between devices with their start and end apart: 7, of which 6 were waited for; matrix products, arithmetic and copies ran while one was open for 5% of the time, Pallas kernels for 0%

commit v1 on v0

--- a/solution.py
+++ b/solution.py
@@ -2,6 +2,10 @@
 import jax.numpy as jnp
 from jax import lax
 from jax.sharding import PartitionSpec as P
+
+
+def recover_table_all(a0):
+    return lax.psum(lax.psum(a0, "rep"), "dom")
 
 
 def encode_block(rows_x, a_inner, a_halo, all_x, halo, w_self, w_nbr, b_enc):
@@ -91,7 +95,7 @@
         jnp.zeros((nodes, width), jnp.float32).at[wanted.reshape(-1)].add(back.reshape(-1, width))
     )
     grad_embed = lax.psum_scatter(local_grad, "rep", scatter_dimension=0, tiled=True)
-    grad_dec1, grad_bias1, grad_dec2 = lax.psum((gw1, gb1, gw2), ("dom", "rep"))
+    grad_dec1, grad_bias1, grad_dec2 = recover_table_all((gw1, gb1, gw2))
     return (embed, grad_embed, grad_dec1, grad_bias1, grad_dec2)
 
 

time: 415 us -> 459 us (1.11)
  the two profiles are of different devices: /device:TPU:23 before, /device:TPU:1 now
where the time goes in v1:
time: 459 us; the launch traced here: 458 us
  blocking collectives  260 us (57%)
  waiting for transfers between devices  95.7 us (21%)
  starting transfers between devices  49.4 us (11%)
  local copies, waits for them, and re-layouts  22.4 us (5%)
  between operations  14.2 us (3%)
  other arithmetic  9.46 us (2%)
  matrix products  6.74 us (1%)
    psum x2, blocking collectives, recover_table_all(): return lax.psum(lax.psum(a0, 'rep'), 'dom')  260 us
    psum x2, waiting for transfers between devices, recover_table_all(): return lax.psum(lax.psum(a0, 'rep'), 'dom')  52.4 us
    all_to_all x1, waiting for transfers between devices, per_device(): lax.all_to_all(embed[wanted], 'dom', split_axis=0, concat_axis=0, tiled=T...  19.5 us
    all_to_all x1, starting transfers between devices, per_device(): lax.all_to_all(halo_rows, 'dom', split_axis=0, concat_axis=0, tiled=True)  18.4 us
    all_to_all x1, waiting for transfers between devices, per_device(): lax.all_to_all(history[lax.all_to_all(halo_rows, 'dom', split_axis=0, con...  12.2 us
    all_to_all x1, starting transfers between devices, per_device(): lax.all_to_all(send_ids, 'dom', split_axis=0, concat_axis=0, tiled=True)  11.6 us
    all_to_all x1, waiting for transfers between devices, per_device(): lax.all_to_all(send_ids, 'dom', split_axis=0, concat_axis=0, tiled=True)  9.41 us
  transfers between devices with their start and end apart: 8, of which 5 were waited for; matrix products, arithmetic and copies ran while one was open for 4% of the time, Pallas kernels for 0%

profile of v1, /device:TPU:1, one launch (start us, length us, event | category | flops | bytes accessed | tf_op | source)
XLA Modules:
  0.0 458.1 jit_solution(6698185986009296410)
XLA Ops:
  7.2 1.6 copy.30
  8.8 18.4 %all-to-all-start = ((s32[128,1,2]{2,1,0:T(1,128)}), s32[128,1,2]{2,1,0:T(1,128)S(1)}, u32[]{:S(2)}, u32[]{:S(2)}) async-start(s32[128,1,2]{2,1,0:T(1,128)} %bitcast), calls=%async_computation | async-start | bytes 131072 | tf_op jit(solution)/shard_map/all_to_all | solution.py:67
  30.0 1.7 fusion.21
  31.8 1.3 fusion.20
  33.4 2.4 scatter_custom_fusion
  36.5 2.1 all-to-all-done
  38.6 11.6 %all-to-all-start.2 = ((s32[128,1,8]{2,1,0:T(1,128)}), s32[128,1,8]{2,1,0:T(1,128)S(1)}, u32[]{:S(2)}, u32[]{:S(2)}) async-start(s32[128,1,8]{2,1,0:T(1,128)} %bitcast.8), calls=%async_computation.2 | async-start | bytes 131072 | tf_op jit(solution)/shard_map/all_to_all | solution.py:84
  50.4 1.2 gather_fusion
  52.3 9.4 %all-to-all-done.2 = s32[128,1,8]{2,1,0:T(1,128)S(1)} async-done(((s32[128,1,8]{2,1,0:T(1,128)}), s32[128,1,8]{2,1,0:T(1,128)S(1)}, u32[]{:S(2)}, u32[]{:S(2)}) %all-to-all-start.2) | async-done | bytes 4128 | tf_op jit(solution)/shard_map/all_to_all | solution.py:84
  61.7 5.7 %all-to-all-start.1 = ((bf16[128,2,256]{2,1,0:T(2,128)(2,1)}), bf16[128,2,256]{2,1,0:T(2,128)(2,1)S(1)}, u32[]{:S(2)}, u32[]{:S(2)}) async-start(bf16[128,2,256]{2,1,0:T(2,128)(2,1)} %reshape.196), calls=%async_computation.1 | async-start | bytes 262144 | tf_op jit(solution)/shard_map/all_to_all | solution.py:66
  67.6 12.2 %all-to-all-done.1 = bf16[128,2,256]{2,1,0:T(2,128)(2,1)S(1)} async-done(((bf16[128,2,256]{2,1,0:T(2,128)(2,1)}), bf16[128,2,256]{2,1,0:T(2,128)(2,1)S(1)}, u32[]{:S(2)}, u32[]{:S(2)}) %all-to-all-start.1) | async-done | bytes 131104 | tf_op jit(solution)/shard_map/all_to_all | solution.py:66
  79.8 2.2 fusion.3
  82.0 4.9 %gather_fusion.1 = bf16[1024,256]{1,0:T(8,128)(2,1)} fusion(bf16[1024,256]{1,0:T(8,128)(2,1)S(1)} %fusion.3, s32[1024]{0:T(1024)S(1)} %broadcast_clamp_fusion), kind=kCustom, calls=%fused_computation.1 | custom fusion | bytes 1052672 | tf_op jit(solution)/shard_map/gather | solution.py:85
  87.0 6.4 %all-to-all-start.3 = ((bf16[128,8,256]{2,1,0:T(8,128)(2,1)}), bf16[128,8,256]{2,1,0:T(8,128)(2,1)S(1)}, u32[]{:S(2)}, u32[]{:S(2)}) async-start(bf16[128,8,256]{2,1,0:T(8,128)(2,1)} %bitcast.11), calls=%async_computation.3 | async-start | bytes 1048576 | tf_op jit(solution)/shard_map/all_to_all | solution.py:85
  93.4 19.5 %all-to-all-done.3 = bf16[128,8,256]{2,1,0:T(8,128)(2,1)S(1)} async-done(((bf16[128,8,256]{2,1,0:T(8,128)(2,1)}), bf16[128,8,256]{2,1,0:T(8,128)(2,1)S(1)}, u32[]{:S(2)}, u32[]{:S(2)}) %all-to-all-start.3) | async-done | bytes 524320 | tf_op jit(solution)/shard_map/all_to_all | solution.py:85
  113.0 1.9 gather_fusion.2
  117.1 3.3 scatter_custom_fusion.1
  120.4 7.1 %all-to-all-start.4 = ((f32[128,8,256]{2,1,0:T(8,128)}), f32[128,8,256]{2,1,0:T(8,128)S(1)}, u32[]{:S(2)}, u32[]{:S(2)}) async-start(f32[128,8,256]{2,1,0:T(8,128)} %bitcast.73), calls=%async_computation.4 | async-start | bytes 2097152 | tf_op jit(solution)/shard_map/all_to_all | solution.py:91
  127.6 0.9 fusion.23
  130.0 52.4 %all-reduce.5.cloned.1.call-done = f32[256,256]{1,0:T(8,128)} async-done(((f32[256,256]{1,0:T(8,128)}), f32[256,256]{1,0:T(8,128)}) %all-reduce.5.cloned.1.call-update) | async-done | bytes 262160 | tf_op jit(solution)/shard_map/psum | solution.py:8
  182.6 7.1 %scatter_custom_fusion.2 = f32[1024,256]{1,0:T(8,128)} fusion(s32[1024]{0:T(1024)S(1)} %bitcast.84, f32[128,8,256]{2,1,0:T(8,128)S(1)} %all-to-all-done.4, f32[]{:T(128)} %constant.8.clone.1), kind=kCustom, calls=%fused_computation.14 | custom fusion | flops 262144 | bytes 2097156 | tf_op jit(solution)/shard_map/scatter-add | solution.py:95
  189.7 7.6 %all-reduce.1 = (f32[256]{0:T(256)S(1)}, f32[256]{0:T(256)S(1)}) all-reduce(f32[256]{0:T(256)S(1)} %get-tuple-element.9, f32[256]{0:T(256)S(1)} %get-tuple-element.15), channel_id=1, replica_groups=mesh['dom'=128,'rep'=4] {'rep'}, use_global_device_ids=true, to_apply=%region_10.11 | all-reduce | flops 512 | bytes 4096 | tf_op jit(solution)/shard_map/psum | solution.py:8
  197.3 252.6 %all-reduce = (f32[256]{0:T(256)}, f32[256]{0:T(256)}) all-reduce(f32[256]{0:T(256)S(1)} %get-tuple-element.7, f32[256]{0:T(256)S(1)} %get-tuple-element.8), channel_id=1, replica_groups=mesh['dom'=128,'rep'=4] {'dom'}, use_global_device_ids=true, to_apply=%region_11.12 | all-reduce | flops 512 | bytes 4096 | tf_op jit(solution)/shard_map/psum | solution.py:8
  449.9 1.7 copy.57
  (81 shorter events, 8.6 us)
Async XLA Ops:
  7.2 22.8 %copy-start = (bf16[1024,1024]{1,0:T(8,128)(2,1)S(1)}, bf16[1024,1024]{1,0:T(8,128)(2,1)}, u32[]{:S(2)}) copy-start(bf16[1024,1024]{1,0:T(8,128)(2,1)} %param.16) | copy-start | bytes 6291460
  7.2 22.8 %copy-start.4 = (bf16[1024,256]{1,0:T(8,128)(2,1)S(1)}, bf16[1024,256]{1,0:T(8,128)(2,1)}, u32[]{:S(2)}) copy-start(bf16[1024,256]{1,0:T(8,128)(2,1)} %param.14) | copy-start | bytes 1572868
  8.8 29.9 %all-to-all-start = ((s32[128,1,2]{2,1,0:T(1,128)}), s32[128,1,2]{2,1,0:T(1,128)S(1)}, u32[]{:S(2)}, u32[]{:S(2)}) async-start(s32[128,1,2]{2,1,0:T(1,128)} %bitcast), calls=%async_computation | async-start | bytes 131072 | tf_op jit(solution)/shard_map/all_to_all | solution.py:67
  30.0 1.8 copy-start.5
  30.0 1.8 copy-start.6
  30.0 3.1 copy-start.8
  31.7 18.7 %copy-start.2 = (bf16[1024,256]{1,0:T(8,128)(2,1)S(1)}, bf16[1024,256]{1,0:T(8,128)(2,1)}, u32[]{:S(2)}) copy-start(bf16[1024,256]{1,0:T(8,128)(2,1)} %param.15) | copy-start | bytes 1572868
  31.8 48.1 %copy-start.3 = (bf16[1024,256]{1,0:T(8,128)(2,1)S(1)}, bf16[1024,256]{1,0:T(8,128)(2,1)}, u32[]{:S(2)}) copy-start(bf16[1024,256]{1,0:T(8,128)(2,1)} %param.17) | copy-start | bytes 1572868
  31.8 48.1 %copy-start.9 = (f32[256]{0:T(256)S(1)}, f32[256]{0:T(256)}, u32[]{:S(2)}) copy-start(f32[256]{0:T(256)} %param.21) | copy-start | bytes 3076
  38.6 23.1 %all-to-all-start.2 = ((s32[128,1,8]{2,1,0:T(1,128)}), s32[128,1,8]{2,1,0:T(1,128)S(1)}, u32[]{:S(2)}, u32[]{:S(2)}) async-start(s32[128,1,8]{2,1,0:T(1,128)} %bitcast.8), calls=%async_computation.2 | async-start | bytes 131072 | tf_op jit(solution)/shard_map/all_to_all | solution.py:84
  61.7 18.0 %all-to-all-start.1 = ((bf16[128,2,256]{2,1,0:T(2,128)(2,1)}), bf16[128,2,256]{2,1,0:T(2,128)(2,1)S(1)}, u32[]{:S(2)}, u32[]{:S(2)}) async-start(bf16[128,2,256]{2,1,0:T(2,128)(2,1)} %reshape.196), calls=%async_computation.1 | async-start | bytes 262144 | tf_op jit(solution)/shard_map/all_to_all | solution.py:66
  82.0 5.0 %copy-start.1 = (bf16[1024,256]{1,0:T(8,128)(2,1)}, bf16[1024,256]{1,0:T(8,128)(2,1)S(1)}, u32[]{:S(2)}) copy-start(bf16[1024,256]{1,0:T(8,128)(2,1)S(1)} %fusion.3) | copy-start | bytes 1572868
  82.0 11.4 %copy-start.12 = (bf16[256]{0:T(256)(128)(2,1)S(1)}, bf16[256]{0:T(256)(128)(2,1)}, u32[]{:S(2)}) copy-start(bf16[256]{0:T(256)(128)(2,1)} %param.27) | copy-start | bytes 1540
  87.0 26.0 %all-to-all-start.3 = ((bf16[128,8,256]{2,1,0:T(8,128)(2,1)}), bf16[128,8,256]{2,1,0:T(8,128)(2,1)S(1)}, u32[]{:S(2)}, u32[]{:S(2)}) async-start(bf16[128,8,256]{2,1,0:T(8,128)(2,1)} %bitcast.11), calls=%async_computation.3 | async-start | bytes 1048576 | tf_op jit(solution)/shard_map/all_to_all | solution.py:85
  113.0 2.5 copy-start.7
  113.0 2.5 copy-start.11
  114.9 1.0 copy-start.10
  120.4 62.1 %all-to-all-start.4 = ((f32[128,8,256]{2,1,0:T(8,128)}), f32[128,8,256]{2,1,0:T(8,128)S(1)}, u32[]{:S(2)}, u32[]{:S(2)}) async-start(f32[128,8,256]{2,1,0:T(8,128)} %bitcast.73), calls=%async_computation.4 | async-start | bytes 2097152 | tf_op jit(solution)/shard_map/all_to_all | solution.py:91
  127.5 54.9 %all-reduce.5.cloned.1.call-start = ((), (), s32[]{:S(2)}) async-start(), calls=%async_computation.7 | async-start | bytes 524288 | tf_op jit(solution)/shard_map/psum | solution.py:8
  128.6 321.3 %all-reduce.7.cloned.1.call-start = ((), (), s32[]{:S(2)}) async-start(), calls=%async_computation.8 | async-start | bytes 524288 | tf_op jit(solution)/shard_map/psum | solution.py:8
  182.5 267.4 %reduce-scatter.2.cloned.1.call-start = ((), (), s32[]{:S(2)}) async-start(), calls=%async_computation.6 | async-start | bytes 1310720 | tf_op jit(solution)/shard_map/reduce_scatter | solution.py:97
Sparse Core Ops, SparseCore 0:
  131.3 51.1 all-reduce.4
  186.0 191.5 all-reduce.6
  381.3 25.3 reduce-scatter.1
